TPU v7x, 32 devices: a whole 2x2x4 slice. The times are simulated.
32 devices in a mesh: row: 16 (over z, y, x), col: 2 (over core).
Axes of the slice: x: 2, y: 2, z: 4, core: 2. Of those that a mesh axis runs over, the one named last changes fastest.
Arguments:
- sim_points: float32 [64, 4096], P(None, 'row'), may hold values from -34 to 34
- obs_points: float32 [64, 4096], P(None, ('row', 'col')), may hold values from -16 to 16
- sim_logw: float32 [4096], P('row'), may hold values from -2.5 to 2.5
- obs_logw: float32 [4096], P(('row', 'col')), may hold values from -2.5 to 2.5
Outputs:
- potential_f: float32 [4096], P('row')
- potential_g: float32 [4096], P(('row', 'col'))
- transport_cost: float32 [1], replicated
All inputs are finite; a program needn't handle non-finite values.
Results may differ from a plain program's by a relative error of at most 0.0003.
Values sent between devices are 32-bit elements; how exact they have to be, the bound alone decides.
A program may use at most 64 MiB of HBM per device.

v0:
```python
import math
import jax
import jax.numpy as jnp
from jax import lax
from jax.sharding import PartitionSpec as P

ITERS = 8
epsilon = 0.05


def joined(value, axis, join):
    pieces = jax.tree.map(lambda part: lax.all_gather(part, axis), value)
    head = jax.tree.map(lambda part: part[0], pieces)
    tail = jax.tree.map(lambda part: part[1:], pieces)
    total, _ = lax.scan(lambda total, piece: (join(total, piece), None), head, tail)
    return total


def pair_cost(points, observed):
    feature_count = points.shape[0]
    sq_points = jnp.sum(points * points, 0)
    sq_observed = jnp.sum(observed * observed, 0)
    inner_products = lax.dot_general(
        points,
        observed,
        (((0,), (0,)), ((), ())),
        precision=lax.Precision.HIGHEST,
        preferred_element_type=jnp.float32,
    )
    return (sq_points[:, None] + sq_observed[None, :] - 2.0 * inner_products) / feature_count


def lse_combine(first, second):
    new_top = jnp.maximum(first[0], second[0])
    return (
        new_top,
        first[1] * jnp.exp(first[0] - new_top) + second[1] * jnp.exp(second[0] - new_top),
    )


def on_device(sim_points, obs_points, sim_logw, obs_logw):
    row_count = lax.axis_size("row")
    obs_dev = obs_points.shape[1]
    total_sim = sim_points.shape[1] * row_count
    total_obs = obs_dev * row_count * lax.axis_size("col")
    observed, logw_all = (
        lax.all_gather(obs_points, "row", axis=1, tiled=True),
        lax.all_gather(obs_logw, "row", axis=0, tiled=True),
    )
    log_a = sim_logw - math.log(total_sim)
    log_b_all = logw_all - math.log(total_obs)
    own_index = lax.axis_index("row")
    resident = pair_cost(sim_points, observed)

    def costs():
        return resident

    potential_g = jnp.zeros((observed.shape[1],), jnp.float32)
    potential_g_own = jnp.zeros((obs_dev,), jnp.float32)
    potential_f = jnp.zeros((sim_points.shape[1],), jnp.float32)
    for iteration in range(ITERS):
        scores = (potential_g[None, :] - costs()) / epsilon
        row_top = jnp.max(scores, 1)
        row_mass = jnp.sum(jnp.exp(scores - row_top[:, None]), 1)
        row_top, row_mass = joined((row_top, row_mass), "col", lse_combine)
        potential_f = epsilon * log_a - epsilon * (row_top + jnp.log(row_mass))
        scores = (potential_f[:, None] - costs()) / epsilon
        col_top = jnp.max(scores, 0)
        col_mass = jnp.sum(jnp.exp(scores - col_top[None, :]), 0)
        col_top, col_mass = joined((col_top, col_mass), "row", lse_combine)
        potential_g = epsilon * log_b_all - epsilon * (col_top + jnp.log(col_mass))
        potential_g_own = lax.dynamic_slice_in_dim(potential_g, own_index * obs_dev, obs_dev)
    costs_tile = costs()
    transport = jnp.exp((potential_f[:, None] + potential_g[None, :] - costs_tile) / epsilon)
    total_cost = lax.psum(jnp.sum(transport * costs_tile), ("row", "col"))
    return (potential_f, potential_g_own, jnp.reshape(total_cost, (1,)))


def solution(mesh):
    in_specs = (P(None, "row"), P(None, ("row", "col")), P("row"), P(("row", "col")))
    out_specs = (P("row"), P(("row", "col")), P())
    return jax.shard_map(
        on_device, mesh=mesh, in_specs=in_specs, out_specs=out_specs, check_vma=False
    )
```

profile of v0, /device:TPU:14, one launch (start us, length us, event | category | flops | bytes accessed | tf_op | source)
XLA Modules:
  0.0 770.5 jit_solution(11684991094862416299)
XLA Ops:
  0.6 31.2 %all_gather.199 = f32[64,2048]{1,0:T(8,128)S(1)} all-gather(f32[64,128]{1,0:T(8,128)} %param.21), channel_id=1, replica_groups=mesh['row'=16,'col'=2] {'row'}, dimensions={1}, use_global_device_ids=true | all-gather | bytes 557056 | tf_op jit(solution)/shard_map/all_gather | solution.py:47
  31.9 0.9 multiply_reduce_fusion.2
  32.8 3.2 fusion.2
  35.9 38.6 %all-gather.32 = f32[16,1,128]{2,1,0:T(1,128)S(1)} all-gather(f32[1,1,128]{2,1,0:T(1,128)S(1)} %bitcast.173), channel_id=1, replica_groups=mesh['row'=16,'col'=2] {'row'}, dimensions={0}, use_global_device_ids=true | all-gather | bytes 8704 | tf_op jit(solution)/shard_map/all_gather | solution.py:48
  75.1 1.8 all-gather.34
  76.9 1.8 all-gather.33
  79.0 36.1 %all-gather.2 = f32[32768]{0:T(1024)S(1)} all-gather(f32[2048]{0:T(1024)S(1)} %fusion.3), channel_id=4, replica_groups=mesh['row'=16,'col'=2] {'row'}, dimensions={0}, use_global_device_ids=true | all-gather | bytes 139264 | tf_op jit(solution)/shard_map/all_gather | solution.py:12
  115.6 38.2 %all-gather.3 = f32[32768]{0:T(1024)S(1)} all-gather(f32[2048]{0:T(1024)S(1)} %exponential_reduce_fusion.14), channel_id=5, replica_groups=mesh['row'=16,'col'=2] {'row'}, dimensions={0}, use_global_device_ids=true | all-gather | bytes 139264 | tf_op jit(solution)/shard_map/all_gather | solution.py:12
  153.9 0.9 while.16
  155.7 1.8 all-gather.36
  157.5 1.8 all-gather.35
  159.6 36.1 %all-gather.6 = f32[32768]{0:T(1024)S(1)} all-gather(f32[2048]{0:T(1024)S(1)} %fusion.5), channel_id=8, replica_groups=mesh['row'=16,'col'=2] {'row'}, dimensions={0}, use_global_device_ids=true | all-gather | bytes 139264 | tf_op jit(solution)/shard_map/all_gather | solution.py:12
  196.2 38.2 %all-gather.7 = f32[32768]{0:T(1024)S(1)} all-gather(f32[2048]{0:T(1024)S(1)} %exponential_reduce_fusion.12), channel_id=9, replica_groups=mesh['row'=16,'col'=2] {'row'}, dimensions={0}, use_global_device_ids=true | all-gather | bytes 139264 | tf_op jit(solution)/shard_map/all_gather | solution.py:12
  234.4 0.9 while.17
  235.7 0.5 exponential_reduce_fusion.11
  236.2 1.8 all-gather.38
  238.0 1.8 all-gather.37
  240.1 36.1 %all-gather.10 = f32[32768]{0:T(1024)S(1)} all-gather(f32[2048]{0:T(1024)S(1)} %fusion.7), channel_id=12, replica_groups=mesh['row'=16,'col'=2] {'row'}, dimensions={0}, use_global_device_ids=true | all-gather | bytes 139264 | tf_op jit(solution)/shard_map/all_gather | solution.py:12
  276.8 38.2 %all-gather.11 = f32[32768]{0:T(1024)S(1)} all-gather(f32[2048]{0:T(1024)S(1)} %exponential_reduce_fusion.10), channel_id=13, replica_groups=mesh['row'=16,'col'=2] {'row'}, dimensions={0}, use_global_device_ids=true | all-gather | bytes 139264 | tf_op jit(solution)/shard_map/all_gather | solution.py:12
  315.0 0.9 while.18
  316.8 1.8 all-gather.40
  318.6 1.8 all-gather.39
  320.7 36.1 %all-gather.14 = f32[32768]{0:T(1024)S(1)} all-gather(f32[2048]{0:T(1024)S(1)} %fusion.9), channel_id=16, replica_groups=mesh['row'=16,'col'=2] {'row'}, dimensions={0}, use_global_device_ids=true | all-gather | bytes 139264 | tf_op jit(solution)/shard_map/all_gather | solution.py:12
  357.3 38.2 %all-gather.15 = f32[32768]{0:T(1024)S(1)} all-gather(f32[2048]{0:T(1024)S(1)} %exponential_reduce_fusion.8), channel_id=17, replica_groups=mesh['row'=16,'col'=2] {'row'}, dimensions={0}, use_global_device_ids=true | all-gather | bytes 139264 | tf_op jit(solution)/shard_map/all_gather | solution.py:12
  395.6 0.9 while.19
  397.4 1.8 all-gather.42
  399.2 1.8 all-gather.41
  401.3 36.1 %all-gather.18 = f32[32768]{0:T(1024)S(1)} all-gather(f32[2048]{0:T(1024)S(1)} %fusion.11), channel_id=20, replica_groups=mesh['row'=16,'col'=2] {'row'}, dimensions={0}, use_global_device_ids=true | all-gather | bytes 139264 | tf_op jit(solution)/shard_map/all_gather | solution.py:12
  437.9 38.3 %all-gather.19 = f32[32768]{0:T(1024)S(1)} all-gather(f32[2048]{0:T(1024)S(1)} %exponential_reduce_fusion.6), channel_id=21, replica_groups=mesh['row'=16,'col'=2] {'row'}, dimensions={0}, use_global_device_ids=true | all-gather | bytes 139264 | tf_op jit(solution)/shard_map/all_gather | solution.py:12
  476.3 0.9 while.20
  478.1 1.8 all-gather.44
  479.9 1.8 all-gather.43
  482.0 36.2 %all-gather.22 = f32[32768]{0:T(1024)S(1)} all-gather(f32[2048]{0:T(1024)S(1)} %fusion.13), channel_id=24, replica_groups=mesh['row'=16,'col'=2] {'row'}, dimensions={0}, use_global_device_ids=true | all-gather | bytes 139264 | tf_op jit(solution)/shard_map/all_gather | solution.py:12
  518.8 38.1 %all-gather.23 = f32[32768]{0:T(1024)S(1)} all-gather(f32[2048]{0:T(1024)S(1)} %exponential_reduce_fusion.4), channel_id=25, replica_groups=mesh['row'=16,'col'=2] {'row'}, dimensions={0}, use_global_device_ids=true | all-gather | bytes 139264 | tf_op jit(solution)/shard_map/all_gather | solution.py:12
  556.9 0.9 while.21
  558.7 1.8 all-gather.46
  560.5 1.8 all-gather.45
  562.6 36.2 %all-gather.26 = f32[32768]{0:T(1024)S(1)} all-gather(f32[2048]{0:T(1024)S(1)} %fusion.15), channel_id=28, replica_groups=mesh['row'=16,'col'=2] {'row'}, dimensions={0}, use_global_device_ids=true | all-gather | bytes 139264 | tf_op jit(solution)/shard_map/all_gather | solution.py:12
  599.3 38.1 %all-gather.27 = f32[32768]{0:T(1024)S(1)} all-gather(f32[2048]{0:T(1024)S(1)} %exponential_reduce_fusion.2), channel_id=29, replica_groups=mesh['row'=16,'col'=2] {'row'}, dimensions={0}, use_global_device_ids=true | all-gather | bytes 139264 | tf_op jit(solution)/shard_map/all_gather | solution.py:12
  637.5 0.9 while.22
  639.3 1.8 all-gather.48
  641.1 1.8 all-gather.47
  643.2 36.2 %all-gather.30 = f32[32768]{0:T(1024)S(1)} all-gather(f32[2048]{0:T(1024)S(1)} %fusion.17), channel_id=32, replica_groups=mesh['row'=16,'col'=2] {'row'}, dimensions={0}, use_global_device_ids=true | all-gather | bytes 139264 | tf_op jit(solution)/shard_map/all_gather | solution.py:12
  679.9 38.1 %all-gather.31 = f32[32768]{0:T(1024)S(1)} all-gather(f32[2048]{0:T(1024)S(1)} %exponential_reduce_fusion), channel_id=33, replica_groups=mesh['row'=16,'col'=2] {'row'}, dimensions={0}, use_global_device_ids=true | all-gather | bytes 139264 | tf_op jit(solution)/shard_map/all_gather | solution.py:12
  718.1 0.9 while.23
  719.0 0.6 dynamic_slice.85
  719.6 1.6 multiply_reduce_fusion
  721.2 49.3 %psum.7 = f32[1]{0:T(128)} all-reduce(f32[1]{0:T(128)} %bitcast.66), channel_id=1, replica_groups=mesh['row'=16,'col'=2] {'row','col'}, use_global_device_ids=true, to_apply=%region_51.52 | all-reduce | flops 1 | bytes 8 | tf_op jit(solution)/shard_map/psum | solution.py:75
  (358 shorter events, 16.9 us)
Async XLA Ops:
  31.8 4.1 copy-start.2
  32.8 45.9 %copy-start = (f32[256]{0:T(256)S(1)}, f32[256]{0:T(256)}, u32[]{:S(2)}) copy-start(f32[256]{0:T(256)} %param.22) | copy-start | bytes 3076
  642.9 76.8 %copy-start.1 = (f32[256]{0:T(256)}, f32[256]{0:T(256)S(1)}, u32[]{:S(2)}) copy-start(f32[256]{0:T(256)S(1)} %multiply_subtract_fusion.8) | copy-start | bytes 3076
where the time goes:
time: 771 us
  blocking collectives  742 us (96%)
  other arithmetic  17 us (2%)
    all_gather x32, blocking collectives, joined(): pieces = jax.tree.map(lambda part: lax.all_gather(part, axis), value)  623 us
    psum x1, blocking collectives, on_device(): total_cost = lax.psum(jnp.sum(transport * costs_tile), ('row', 'col'))  49.3 us
    all_gather x1, blocking collectives, on_device(): lax.all_gather(obs_logw, 'row', axis=0, tiled=True)  38.6 us
    all_gather x1, blocking collectives, on_device(): lax.all_gather(obs_points, 'row', axis=1, tiled=True)  31.2 us

commit v1 on v0

--- a/solution.py
+++ b/solution.py
@@ -6,6 +6,22 @@
 
 ITERS = 8
 epsilon = 0.05
+
+
+def rest_sides(mat, net_axis="row"):
+    workers = lax.axis_size(net_axis)
+    steps_seen = [mat]
+    for j0 in range(1, workers):
+        steps_seen.append(
+            lax.ppermute(
+                steps_seen[j0 - 1],
+                net_axis,
+                perm=[(hop_no, (hop_no - 1) % workers) for hop_no in range(workers)],
+            )
+        )
+    local_now = jnp.concatenate(steps_seen, axis=1)
+    parts_out = jnp.roll(local_now, lax.axis_index(net_axis) * mat.shape[1], axis=1)
+    return parts_out
 
 
 def joined(value, axis, join):
@@ -44,7 +60,7 @@
     total_sim = sim_points.shape[1] * row_count
     total_obs = obs_dev * row_count * lax.axis_size("col")
     observed, logw_all = (
-        lax.all_gather(obs_points, "row", axis=1, tiled=True),
+        rest_sides(obs_points),
         lax.all_gather(obs_logw, "row", axis=0, tiled=True),
     )
     log_a = sim_logw - math.log(total_sim)

time: 771 us -> 842 us (1.092)
  waiting for transfers between devices: 0 us -> 76.7 us
  blocking collectives: 742 us -> 728 us
    ppermute x0 -> x15, waiting for transfers between devices: none -> 76.7 us  [rest_sides(): lax.ppermute(steps_seen[j0 - 1], net_axis, perm=[(hop_no, (hop_no - 1) %...]
    all_gather x1 -> x0, blocking collectives: 31.2 us -> none  [on_device(): lax.all_gather(obs_points, 'row', axis=1, tiled=True)]
    all_gather x32, blocking collectives: 623 us -> 648 us  [joined(): pieces = jax.tree.map(lambda part: lax.all_gather(part, axis), value)]
  transfers between devices with their start and end apart: 0 -> 15, of which waited for: 0 -> 14; matrix products, arithmetic and copies ran while one was open for 0% -> 0% of each run, Pallas kernels for 0% -> 0%
where the time goes in v1:
time: 842 us
  blocking collectives  728 us (86%)
  waiting for transfers between devices  76.7 us (9%)
  other arithmetic  19.9 us (2%)
    all_gather x32, blocking collectives, joined(): pieces = jax.tree.map(lambda part: lax.all_gather(part, axis), value)  648 us
    ppermute x15, waiting for transfers between devices, rest_sides(): lax.ppermute(steps_seen[j0 - 1], net_axis, perm=[(hop_no, (hop_no - 1) %...  76.7 us
    psum x1, blocking collectives, on_device(): total_cost = lax.psum(jnp.sum(transport * costs_tile), ('row', 'col'))  49.4 us
    all_gather x1, blocking collectives, on_device(): lax.all_gather(obs_logw, 'row', axis=0, tiled=True)  30.8 us
  transfers between devices with their start and end apart: 15, of which 14 were waited for; matrix products, arithmetic and copies ran while one was open for 0% of the time, Pallas kernels for 0%

profile of v1, /device:TPU:14, one launch (start us, length us, event | category | flops | bytes accessed | tf_op | source)
XLA Modules:
  0.0 841.5 jit_solution(17609358861868873248)
XLA Ops:
  2.1 30.8 %all-gather.32 = f32[16,1,128]{2,1,0:T(1,128)S(1)} all-gather(f32[1,1,128]{2,1,0:T(1,128)} %bitcast.178), channel_id=1, replica_groups=mesh['row'=16,'col'=2] {'row'}, dimensions={0}, use_global_device_ids=true | all-gather | bytes 8704 | tf_op jit(solution)/shard_map/all_gather | solution.py:64
  34.3 5.1 collective-permute-done.1
  40.9 4.2 collective-permute-done.2
  45.7 5.1 collective-permute-done.3
  50.8 5.7 collective-permute-done.4
  56.5 5.7 collective-permute-done.5
  62.3 5.7 collective-permute-done.6
  68.0 5.7 collective-permute-done.7
  73.7 5.7 collective-permute-done.8
  79.4 5.7 collective-permute-done.9
  85.1 5.9 collective-permute-done.10
  91.1 5.7 collective-permute-done.11
  96.8 5.7 collective-permute-done.12
  102.5 5.7 collective-permute-done.13
  108.9 5.0 collective-permute-done.14
  114.9 2.4 fusion.3
  117.8 1.8 all-gather.34
  119.6 1.8 all-gather.33
  122.6 57.7 %all-gather.2 = f32[32768]{0:T(1024)S(1)} all-gather(f32[2048]{0:T(1024)S(1)} %fusion.4), channel_id=4, replica_groups=mesh['row'=16,'col'=2] {'row'}, dimensions={0}, use_global_device_ids=true | all-gather | bytes 139264 | tf_op jit(solution)/shard_map/all_gather | solution.py:28
  180.3 41.7 %all-gather.3 = f32[32768]{0:T(1024)S(1)} all-gather(f32[2048]{0:T(1024)S(1)} %exponential_reduce_fusion.14), channel_id=5, replica_groups=mesh['row'=16,'col'=2] {'row'}, dimensions={0}, use_global_device_ids=true | all-gather | bytes 139264 | tf_op jit(solution)/shard_map/all_gather | solution.py:28
  224.0 1.8 all-gather.36
  225.8 1.8 all-gather.35
  228.7 36.2 %all-gather.6 = f32[32768]{0:T(1024)S(1)} all-gather(f32[2048]{0:T(1024)S(1)} %fusion.6), channel_id=8, replica_groups=mesh['row'=16,'col'=2] {'row'}, dimensions={0}, use_global_device_ids=true | all-gather | bytes 139264 | tf_op jit(solution)/shard_map/all_gather | solution.py:28
  264.9 38.1 %all-gather.7 = f32[32768]{0:T(1024)S(1)} all-gather(f32[2048]{0:T(1024)S(1)} %exponential_reduce_fusion.12), channel_id=9, replica_groups=mesh['row'=16,'col'=2] {'row'}, dimensions={0}, use_global_device_ids=true | all-gather | bytes 139264 | tf_op jit(solution)/shard_map/all_gather | solution.py:28
  305.0 1.8 all-gather.38
  306.8 1.8 all-gather.37
  309.7 36.1 %all-gather.10 = f32[32768]{0:T(1024)S(1)} all-gather(f32[2048]{0:T(1024)S(1)} %fusion.8), channel_id=12, replica_groups=mesh['row'=16,'col'=2] {'row'}, dimensions={0}, use_global_device_ids=true | all-gather | bytes 139264 | tf_op jit(solution)/shard_map/all_gather | solution.py:28
  345.9 38.3 %all-gather.11 = f32[32768]{0:T(1024)S(1)} all-gather(f32[2048]{0:T(1024)S(1)} %exponential_reduce_fusion.10), channel_id=13, replica_groups=mesh['row'=16,'col'=2] {'row'}, dimensions={0}, use_global_device_ids=true | all-gather | bytes 139264 | tf_op jit(solution)/shard_map/all_gather | solution.py:28
  386.1 1.8 all-gather.40
  387.9 1.8 all-gather.39
  390.9 36.2 %all-gather.14 = f32[32768]{0:T(1024)S(1)} all-gather(f32[2048]{0:T(1024)S(1)} %fusion.10), channel_id=16, replica_groups=mesh['row'=16,'col'=2] {'row'}, dimensions={0}, use_global_device_ids=true | all-gather | bytes 139264 | tf_op jit(solution)/shard_map/all_gather | solution.py:28
  427.1 38.1 %all-gather.15 = f32[32768]{0:T(1024)S(1)} all-gather(f32[2048]{0:T(1024)S(1)} %exponential_reduce_fusion.8), channel_id=17, replica_groups=mesh['row'=16,'col'=2] {'row'}, dimensions={0}, use_global_device_ids=true | all-gather | bytes 139264 | tf_op jit(solution)/shard_map/all_gather | solution.py:28
  467.1 1.8 all-gather.42
  468.9 1.8 all-gather.41
  471.9 36.2 %all-gather.18 = f32[32768]{0:T(1024)S(1)} all-gather(f32[2048]{0:T(1024)S(1)} %fusion.12), channel_id=20, replica_groups=mesh['row'=16,'col'=2] {'row'}, dimensions={0}, use_global_device_ids=true | all-gather | bytes 139264 | tf_op jit(solution)/shard_map/all_gather | solution.py:28
  508.0 38.1 %all-gather.19 = f32[32768]{0:T(1024)S(1)} all-gather(f32[2048]{0:T(1024)S(1)} %exponential_reduce_fusion.6), channel_id=21, replica_groups=mesh['row'=16,'col'=2] {'row'}, dimensions={0}, use_global_device_ids=true | all-gather | bytes 139264 | tf_op jit(solution)/shard_map/all_gather | solution.py:28
  548.1 1.8 all-gather.44
  549.9 1.8 all-gather.43
  552.8 36.2 %all-gather.22 = f32[32768]{0:T(1024)S(1)} all-gather(f32[2048]{0:T(1024)S(1)} %fusion.14), channel_id=24, replica_groups=mesh['row'=16,'col'=2] {'row'}, dimensions={0}, use_global_device_ids=true | all-gather | bytes 139264 | tf_op jit(solution)/shard_map/all_gather | solution.py:28
  589.0 38.1 %all-gather.23 = f32[32768]{0:T(1024)S(1)} all-gather(f32[2048]{0:T(1024)S(1)} %exponential_reduce_fusion.4), channel_id=25, replica_groups=mesh['row'=16,'col'=2] {'row'}, dimensions={0}, use_global_device_ids=true | all-gather | bytes 139264 | tf_op jit(solution)/shard_map/all_gather | solution.py:28
  629.0 1.8 all-gather.46
  630.8 1.8 all-gather.45
  633.8 36.2 %all-gather.26 = f32[32768]{0:T(1024)S(1)} all-gather(f32[2048]{0:T(1024)S(1)} %fusion.16), channel_id=28, replica_groups=mesh['row'=16,'col'=2] {'row'}, dimensions={0}, use_global_device_ids=true | all-gather | bytes 139264 | tf_op jit(solution)/shard_map/all_gather | solution.py:28
  670.0 38.1 %all-gather.27 = f32[32768]{0:T(1024)S(1)} all-gather(f32[2048]{0:T(1024)S(1)} %exponential_reduce_fusion.2), channel_id=29, replica_groups=mesh['row'=16,'col'=2] {'row'}, dimensions={0}, use_global_device_ids=true | all-gather | bytes 139264 | tf_op jit(solution)/shard_map/all_gather | solution.py:28
  710.0 1.8 all-gather.48
  714.8 36.2 %all-gather.30 = f32[32768]{0:T(1024)S(1)} all-gather(f32[2048]{0:T(1024)S(1)} %fusion.18), channel_id=32, replica_groups=mesh['row'=16,'col'=2] {'row'}, dimensions={0}, use_global_device_ids=true | all-gather | bytes 139264 | tf_op jit(solution)/shard_map/all_gather | solution.py:28
  751.0 38.1 %all-gather.31 = f32[32768]{0:T(1024)S(1)} all-gather(f32[2048]{0:T(1024)S(1)} %exponential_reduce_fusion), channel_id=33, replica_groups=mesh['row'=16,'col'=2] {'row'}, dimensions={0}, use_global_device_ids=true | all-gather | bytes 139264 | tf_op jit(solution)/shard_map/all_gather | solution.py:28
  791.6 49.4 %psum.7 = f32[1]{0:T(128)} all-reduce(f32[1]{0:T(128)} %bitcast.67), channel_id=1, replica_groups=mesh['row'=16,'col'=2] {'row','col'}, use_global_device_ids=true, to_apply=%region_51.52 | all-reduce | flops 1 | bytes 8 | tf_op jit(solution)/shard_map/psum | solution.py:91
  (419 shorter events, 38.3 us)
Async XLA Ops:
  0.6 114.3 %copy-start = (f32[64,256]{1,0:T(8,128)S(1)}, f32[64,256]{1,0:T(8,128)}, u32[]{:S(2)}) copy-start(f32[64,256]{1,0:T(8,128)} %param.20) | copy-start | bytes 196612
  0.6 33.0 %collective-permute-start = (f32[64,128]{1,0:T(8,128)}, f32[64,128]{1,0:T(8,128)S(1)}, u32[]{:S(2)}, u32[]{:S(2)}) collective-permute-start(f32[64,128]{1,0:T(8,128)} %param.21), channel_id=1, source_target_pairs={{0,30},{2,0},{4,2},{6,4},{8,6},{10,8},{12,10},{14,12},{16,14},{18,... | collective-permute-start | bytes 98312 | tf_op jit(solution)/shard_map/ppermute | solution.py:16
  33.7 5.7 collective-permute-start.1
  39.4 5.7 collective-permute-start.2
  45.1 5.7 collective-permute-start.3
  50.8 5.7 collective-permute-start.4
  56.5 5.7 collective-permute-start.5
  62.2 5.7 collective-permute-start.6
  68.0 5.7 collective-permute-start.7
  73.7 5.7 collective-permute-start.8
  79.4 5.7 collective-permute-start.9
  85.1 5.9 collective-permute-start.10
  91.0 5.7 collective-permute-start.11
  96.8 5.7 collective-permute-start.12
  102.5 5.7 collective-permute-start.13
  108.2 5.7 collective-permute-start.14
  114.9 6.5 copy-start.1
  713.6 76.5 %copy-start.2 = (f32[256]{0:T(256)}, f32[256]{0:T(256)S(1)}, u32[]{:S(2)}) copy-start(f32[256]{0:T(256)S(1)} %multiply_subtract_fusion.8) | copy-start | bytes 3076
